TPU v7x, 32 devices: a whole 2x2x4 slice. The times are simulated.
32 devices in a mesh: tm: 4 (over x, core), space: 8 (over z, y).
Axes of the slice: x: 2, y: 2, z: 4, core: 2. Of those that a mesh axis runs over, the one named last changes fastest.
Arguments:
- cotangent: bfloat16 [16, 64, 8192], P('tm', 'space'), may hold values from -6 to 6
- saved_mix: bfloat16 [16, 64, 8192], P('tm', 'space'), may hold values from -6 to 6
- saved_pre: bfloat16 [16, 64, 8192], P('tm', 'space'), may hold values from -8 to 8
- kernel_one: bfloat16 [4, 3, 3, 64, 64], replicated, may hold values from -0.25 to 0.25
- kernel_two: bfloat16 [4, 3, 3, 64, 64], replicated, may hold values from -0.25 to 0.25
- ref_pairs: int32 [16, 2], replicated, may hold values from 0 to 15, as said below
- frame_level: int32 [16], replicated, may hold values from 0 to 4, as said below
Outputs:
- input_grad: float32 [16, 64, 8192], P('tm', 'space')
- weight_grad_one: float32 [4, 3, 3, 64, 64], replicated
- weight_grad_two: float32 [4, 3, 3, 64, 64], replicated
Inputs may be any that keep to these rules, and one draw needn't show every extreme that they name: Frame c was predicted from frames ref_pairs[c, 0] and ref_pairs[c, 1]; for a frame of level k >= 1 both have a level below k (at level 1 both name the level-0 frame); the level-0 frame names itself twice. `frame_level`: one frame has level 0 and 2**(k-1) frames have level k for k from 1 to 4; frames are stored in an order drawn from the seed.
All inputs are finite; a program needn't handle non-finite values.
Results may differ from a plain program's by a relative error of at most 0.006.
Values may be sent and summed in bfloat16 or wider, within the bound.
A program may use at most 64 MiB of HBM per device.

v0:
```python
import math
import jax
import jax.numpy as jnp
from jax import lax
from jax.sharding import PartitionSpec as P


def padded_2(cells, sides, width):
    for axis, dim in sides:
        count = lax.axis_size(axis)
        ends = count - 1
        head = lax.slice_in_dim(cells, 0, width, axis=dim)
        tail = lax.slice_in_dim(cells, cells.shape[dim] - width, cells.shape[dim], axis=dim)
        cells = jnp.concatenate(
            [
                lax.ppermute(tail, axis, [(i, (i + 1) % count) for i in range(ends)]),
                cells,
                lax.ppermute(head, axis, [((i + 1) % count, i) for i in range(ends)]),
            ],
            axis=dim,
        )
    return cells


def flipped(kernel):
    return jnp.transpose(kernel[::-1, ::-1], (0, 1, 3, 2))


def pair_kernel(kernel):
    blank = jnp.zeros_like(kernel[:, 0])
    row_blocks = []
    for in_part in range(4):
        col_blocks = []
        for out_half in range(2):
            col_tap = in_part - out_half
            col_blocks.append(kernel[:, col_tap] if 0 <= col_tap <= 2 else blank)
        row_blocks.append(jnp.concatenate(col_blocks, axis=-1))
    return jnp.concatenate(row_blocks, axis=1)


def pair_view(field, channels):
    col_count = field.shape[2] // channels
    grid = field.reshape(field.shape[0], field.shape[1], col_count, channels)
    grid = jnp.pad(grid, ((0, 0), (0, 0), (1, 1), (0, 0)))
    grid = grid.reshape(field.shape[0], field.shape[1], (col_count + 2) // 2, 2 * channels)
    return jnp.concatenate((grid[:, :, :-1], grid[:, :, 1:]), axis=-1)


def conv_taps(field, paired):
    channels = paired.shape[2] // 2
    windows = pair_view(field, channels)
    row_count = field.shape[1] - 2
    result = jnp.einsum(
        "nrjk,kc->nrjc", windows[:, 0:row_count], paired[0], preferred_element_type=jnp.float32
    )
    for row_tap in range(1, 3):
        result = result + jnp.einsum(
            "nrjk,kc->nrjc",
            windows[:, row_tap : row_tap + row_count],
            paired[row_tap],
            preferred_element_type=jnp.float32,
        )
    return result.reshape(field.shape[0], row_count, -1)


def correlate(field, cot, channels):
    windows = pair_view(field, channels)
    row_count = cot.shape[1]
    cot_pairs = cot.reshape(cot.shape[0], row_count, -1, 2 * channels)
    taps = []
    for row_tap in range(3):
        blocks = jnp.einsum(
            "nrjk,nrjc->nkc",
            windows[:, row_tap : row_tap + row_count],
            cot_pairs,
            preferred_element_type=jnp.float32,
        )
        row_taps = []
        for col_tap in range(3):
            first_part = blocks[:, col_tap * channels : (col_tap + 1) * channels, 0:channels]
            second_part = blocks[
                :, (col_tap + 1) * channels : (col_tap + 2) * channels, channels : 2 * channels
            ]
            row_taps.append(first_part + second_part)
        taps.append(jnp.stack(row_taps, axis=1))
    return jnp.stack(taps, axis=1)


def backprop(slot_cot, slot_slope, kernel_inner, kernel_outer):
    padded = padded_2(slot_cot, (("space", 1),), 1)
    slot_grad = (conv_taps(padded, kernel_inner) * slot_slope).astype(jnp.bfloat16)
    grad_padded = padded_2(slot_grad, (("space", 1),), 1)
    to_refs = conv_taps(grad_padded, kernel_outer).astype(jnp.bfloat16)
    return (slot_grad, to_refs)


def body_time(cotangent, saved_mix, saved_pre, kernel_one, kernel_two, ref_pairs, frame_level):
    frames_dev = cotangent.shape[0]
    row_count = cotangent.shape[1]
    channels = kernel_one.shape[-1]
    levels_all = kernel_one.shape[0]
    col_count = cotangent.shape[2] // channels
    first_frame = lax.axis_index("tm") * frames_dev
    local_ids = first_frame + jnp.arange(frames_dev, dtype=jnp.int32)
    local_level = lax.dynamic_slice_in_dim(frame_level, first_frame, frames_dev, 0)
    frame_count = ref_pairs.shape[0]
    all_frames = jnp.arange(frame_count, dtype=jnp.int32)
    preact = saved_pre.astype(jnp.float32)
    sigmoid_pre = jax.nn.sigmoid(preact)
    act_slope = sigmoid_pre * (1.0 + preact * (1.0 - sigmoid_pre))
    act_out = (preact * sigmoid_pre).astype(jnp.bfloat16)
    saved_rims = padded_2(jnp.stack((saved_mix, act_out)), (("space", 2),), 1)
    cot_total = cotangent.astype(jnp.float32)
    kept_grad = jnp.zeros_like(cotangent)
    for level_now in range(levels_all, 0, -1):
        active = local_level == level_now
        slot_count = min(frames_dev, 2 ** (level_now - 1))
        ranks = jnp.cumsum(active.astype(jnp.int32)) - 1
        picker = jnp.logical_and(
            ranks[None, :] == jnp.arange(slot_count, dtype=jnp.int32)[:, None], active[None, :]
        )
        picker_wide = picker.astype(jnp.float32)
        slot_cot = jnp.einsum(
            "sf,fx->sx",
            picker.astype(jnp.bfloat16),
            cot_total.astype(jnp.bfloat16).reshape(frames_dev, -1),
            preferred_element_type=jnp.float32,
        )
        slot_cot = slot_cot.astype(jnp.bfloat16).reshape(slot_count, row_count, -1)
        slot_slope = jnp.einsum(
            "sf,fx->sx",
            picker_wide,
            act_slope.reshape(frames_dev, -1),
            precision=lax.Precision.HIGHEST,
        ).reshape(slot_count, row_count, -1)
        slot_ids = jnp.sum(picker.astype(jnp.int32) * local_ids[None, :], axis=1)
        slot_ok = jnp.sum(picker.astype(jnp.int32), axis=1)
        kernel_inner = pair_kernel(flipped(kernel_two[level_now - 1]))
        kernel_outer = pair_kernel(flipped(kernel_one[level_now - 1]))
        slot_grad, to_refs = backprop(slot_cot, slot_slope, kernel_inner, kernel_outer)
        frame_grad = jnp.einsum(
            "sf,sx->fx",
            picker.astype(jnp.bfloat16),
            slot_grad.reshape(slot_grad.shape[0], -1),
            preferred_element_type=jnp.float32,
        )
        frame_grad = frame_grad.astype(jnp.bfloat16).reshape(kept_grad.shape)
        kept_grad = jnp.where(active[:, None, None], frame_grad, kept_grad)
        moved = lax.all_gather(to_refs, "tm", axis=0, tiled=True)
        sender_ids = lax.all_gather(slot_ids, "tm", axis=0, tiled=True)
        sender_ok = lax.all_gather(slot_ok, "tm", axis=0, tiled=True)
        matches = (sender_ids[:, None] == all_frames[None, :]).astype(jnp.int32)
        first_ref = jnp.sum(matches * ref_pairs[None, :, 0], axis=1)
        second_ref = jnp.sum(matches * ref_pairs[None, :, 1], axis=1)
        hits = (first_ref[:, None] == local_ids[None, :]).astype(jnp.float32) + (
            second_ref[:, None] == local_ids[None, :]
        ).astype(jnp.float32)
        weights = 0.5 * sender_ok[:, None].astype(jnp.float32) * hits
        added = jnp.einsum(
            "kf,kx->fx",
            weights.astype(jnp.bfloat16),
            moved.reshape(moved.shape[0], -1),
            preferred_element_type=jnp.float32,
        )
        cot_total = cot_total + added.reshape(cot_total.shape)
    final_cot = cot_total.astype(jnp.bfloat16)
    per_one = correlate(saved_rims[0], kept_grad, channels)
    per_two = correlate(saved_rims[1], final_cot, channels)
    level_hot = (
        local_level[:, None] == jnp.arange(1, levels_all + 1, dtype=jnp.int32)[None, :]
    ).astype(jnp.float32)
    scale = 1.0 / math.sqrt(row_count * lax.axis_size("space") * col_count)
    sum_one = scale * jnp.sum(level_hot[:, :, None, None, None, None] * per_one[:, None], axis=0)
    sum_two = scale * jnp.sum(level_hot[:, :, None, None, None, None] * per_two[:, None], axis=0)
    weight_one, weight_two = lax.psum((sum_one, sum_two), ("tm", "space"))
    return (cot_total, weight_one, weight_two)


def on_device(cotangent, saved_mix, saved_pre, kernel_one, kernel_two, ref_pairs, frame_level):
    return body_time(
        cotangent, saved_mix, saved_pre, kernel_one, kernel_two, ref_pairs, frame_level
    )


def solution(mesh):
    placed = (
        P("tm", "space", None),
        P("tm", "space", None),
        P("tm", "space", None),
        P(),
        P(),
        P(),
        P(),
    )
    return jax.shard_map(
        on_device,
        mesh=mesh,
        in_specs=placed,
        out_specs=(P("tm", "space", None), P(), P()),
        check_vma=False,
    )
```

profile of v0, /device:TPU:0, one launch (start us, length us, event | category | flops | bytes accessed | tf_op | source)
XLA Modules:
  0.0 384.8 jit_solution(5619695112859020218)
XLA Ops:
  7.2 1.3 broadcast_compare_fusion
  10.0 1.4 copy.215
  13.1 4.9 %collective-permute-start = (bf16[4,1,8192]{2,0,1:T(4,128)(2,1)S(1)}, bf16[4,1,8192]{2,0,1:T(4,128)(2,1)S(1)}, u32[]{:S(2)}, u32[]{:S(2)}) collective-permute-start(bf16[4,1,8192]{2,0,1:T(4,128)(2,1)S(1)} %get-tuple-element.102), channel_id=1, source_target_pairs={{0,1},{1,2},{2,3},{3,4},{4,5},{5,6},{6,7},{8,9},{9,10},{10,11},{11... | collective-permute-start | bytes 196616 | tf_op jit(solution)/shard_map/ppermute | solution.py:16
  18.0 1.3 collective-permute-start.1
  21.1 2.3 fusion.46
  27.4 1.4 select_maximum_fusion.2
  32.2 2.4 fusion
  34.6 4.6 %collective-permute-start.2 = (bf16[4,1,8192]{2,0,1:T(4,128)(2,1)S(1)}, bf16[4,1,8192]{2,0,1:T(4,128)(2,1)S(1)}, u32[]{:S(2)}, u32[]{:S(2)}) collective-permute-start(bf16[4,1,8192]{2,0,1:T(4,128)(2,1)S(1)} %get-tuple-element.100), channel_id=1, source_target_pairs={{0,1},{1,2},{2,3},{3,4},{4,5},{5,6},{6,7},{8,9},{9,10},{10,11},{11... | collective-permute-start | bytes 196616 | tf_op jit(solution)/shard_map/ppermute | solution.py:16
  39.2 1.5 collective-permute-start.3
  41.0 4.7 %collective-permute-done.3 = bf16[4,1,8192]{2,0,1:T(4,128)(2,1)S(1)} collective-permute-done((bf16[4,1,8192]{2,0,1:T(4,128)(2,1)S(1)}, bf16[4,1,8192]{2,0,1:T(4,128)(2,1)S(1)}, u32[]{:S(2)}, u32[]{:S(2)}) %collective-permute-start.3) | collective-permute-done | bytes 65568 | tf_op jit(solution)/shard_map/ppermute | solution.py:18
  46.2 1.9 reshape.439
  48.2 1.8 pad.50
  53.8 1.3 pad_maximum_fusion.21
  55.1 5.7 %collective-permute-start.16 = (bf16[2,4,1,8192]{3,2,1,0:T(2,128)(2,1)}, bf16[2,4,1,8192]{3,2,1,0:T(2,128)(2,1)}, u32[]{:S(2)}, u32[]{:S(2)}) collective-permute-start(bf16[2,4,1,8192]{3,2,1,0:T(2,128)(2,1)} %get-tuple-element.54), channel_id=1, source_target_pairs={{0,1},{1,2},{2,3},{3,4},{4,5},{5,6},{6,7},{8,9},{9,10},{10,11},{11... | collective-permute-start | bytes 393224 | tf_op jit(solution)/shard_map/ppermute | solution.py:16
  60.8 1.3 collective-permute-start.17
  66.2 1.5 dynamic-update-slice.6
  67.7 1.4 dynamic-update-slice.7
  69.0 5.7 %all-reduce.34 = (s32[16]{0:T(128)S(1)}, s32[16]{0:T(128)S(1)}, s32[16]{0:T(128)S(1)}, s32[16]{0:T(128)}, s32[8]{0:T(128)S(1)}, /*index=5*/s32[8]{0:T(128)}, s32[4]{0:T(128)S(1)}, s32[4]{0:T(128)}) all-reduce(s32[16]{0:T(128)S(1)} %dynamic-update-slice.3, s32[16]{0:T(128)S(1)} %dynamic-update-slice.1, ...), channel_id=1, replica_groups=mesh['tm'=4,'space'=8] {'tm'}, use_global_device_ids=true, to_apply=%add.29 | all-reduce | flops 88 | bytes 704
  75.8 2.2 all-gather.4.cloned.1.call-done
  78.1 5.5 %fusion.214 = (bf16[4,8,8192]{2,0,1:T(4,128)(2,1)S(1)}, f32[4,8,8192]{2,0,1:T(4,128)}) fusion(s32[16]{0:T(128)S(1)} %get-tuple-element.31, s32[16]{0:T(128)S(1)} %get-tuple-element.30, f32[16]{0:T(128)S(1)} %convert_multiply_fusion.5, s32[4]{0:T(128)S(1)} %get-tuple-element.160, bf16[4,8,8192]{2,1,0:T(8,128)(2,1)S(1)} %copy-done.31, ...), kind=kOutput, calls=%fused_computation.415 | convolution fusion | flops 9175488 | bytes 4194512 | tf_op jit(solution)/shard_map/kf,kx->fx/dot_general | solution.py:159
  84.2 3.4 collective-permute-start.4
  87.6 1.7 collective-permute-start.5
  91.7 2.0 collective-permute-done.5
  94.5 1.4 select_maximum_fusion
  99.3 2.4 fusion.1
  101.7 4.3 %collective-permute-start.6 = (bf16[4,1,8192]{2,0,1:T(4,128)(2,1)S(1)}, bf16[4,1,8192]{2,0,1:T(4,128)(2,1)S(1)}, u32[]{:S(2)}, u32[]{:S(2)}) collective-permute-start(bf16[4,1,8192]{2,0,1:T(4,128)(2,1)S(1)} %get-tuple-element.96), channel_id=1, source_target_pairs={{0,1},{1,2},{2,3},{3,4},{4,5},{5,6},{6,7},{8,9},{9,10},{10,11},{11... | collective-permute-start | bytes 196616 | tf_op jit(solution)/shard_map/ppermute | solution.py:16
  106.0 1.3 collective-permute-start.7
  107.9 4.3 %collective-permute-done.7 = bf16[4,1,8192]{2,0,1:T(4,128)(2,1)S(1)} collective-permute-done((bf16[4,1,8192]{2,0,1:T(4,128)(2,1)S(1)}, bf16[4,1,8192]{2,0,1:T(4,128)(2,1)S(1)}, u32[]{:S(2)}, u32[]{:S(2)}) %collective-permute-start.7) | collective-permute-done | bytes 65568 | tf_op jit(solution)/shard_map/ppermute | solution.py:18
  112.7 1.9 reshape.447
  114.6 1.8 pad.52
  124.9 2.4 fusion.143
  127.2 15.2 %all-gather.6.cloned.1.call-done = bf16[16,8,8192]{2,1,0:T(8,128)(2,1)} async-done(((bf16[4,8,8192]{2,1,0:T(8,128)(2,1)}), bf16[16,8,8192]{2,1,0:T(8,128)(2,1)}) %all-gather.6.cloned.1.call-update) | async-done | bytes 2097168 | tf_op jit(solution)/shard_map/all_gather | solution.py:149
  142.4 5.2 %fusion.215 = (bf16[4,8,8192]{2,0,1:T(4,128)(2,1)S(1)}, f32[4,8,8192]{2,0,1:T(4,128)}) fusion(f32[4,8,8192]{2,0,1:T(4,128)S(1)} %copy-done.14, s32[16]{0:T(128)S(1)} %get-tuple-element.32, s32[16]{0:T(128)S(1)} %get-tuple-element.29, f32[16]{0:T(128)S(1)} %convert_multiply_fusion.4, s32[4]{0:T(128)S(1)} %get-tuple-element.160, ...), kind=kOutput, calls=%fused_computation.416 | convolution fusion | flops 8913344 | bytes 4718800 | tf_op jit(solution)/shard_map/kf,kx->fx/dot_general | solution.py:159
  148.1 3.4 collective-permute-start.8
  151.5 1.3 collective-permute-start.9
  154.5 2.7 collective-permute-done.9
  159.3 2.0 fusion.2
  161.3 4.3 %collective-permute-start.10 = (bf16[2,1,8192]{2,0,1:T(2,128)(2,1)S(1)}, bf16[2,1,8192]{2,0,1:T(2,128)(2,1)S(1)}, u32[]{:S(2)}, u32[]{:S(2)}) collective-permute-start(bf16[2,1,8192]{2,0,1:T(2,128)(2,1)S(1)} %get-tuple-element.108), channel_id=1, source_target_pairs={{0,1},{1,2},{2,3},{3,4},{4,5},{5,6},{6,7},{8,9},{9,10},{10,11},{11... | collective-permute-start | bytes 98312 | tf_op jit(solution)/shard_map/ppermute | solution.py:16
  165.6 1.5 collective-permute-start.11
  167.1 2.0 pad_maximum_fusion
  169.1 2.2 collective-permute-done.11
  171.9 1.3 reshape.455
  173.2 1.3 pad.54
  176.8 1.1 fusion.193
  178.5 1.1 reshape_squeeze.7
  181.8 1.9 reshape_squeeze.6
  183.7 1.8 pad.57
  186.3 1.3 fusion.195
  187.6 1.3 fusion.194
  189.4 3.3 all-gather.8.cloned.1.call-done
  192.7 2.7 fusion.216
  196.0 3.4 collective-permute-start.12
  199.4 1.5 collective-permute-start.13
  201.9 3.3 collective-permute-done.13
  211.1 4.3 %collective-permute-start.14 = (bf16[1,1,8192]{2,1,0:T(2,128)(2,1)S(1)}, bf16[1,1,8192]{2,1,0:T(2,128)(2,1)S(1)}, u32[]{:S(2)}, u32[]{:S(2)}) collective-permute-start(bf16[1,1,8192]{2,1,0:T(2,128)(2,1)S(1)} %get-tuple-element.140), channel_id=1, source_target_pairs={{0,1},{1,2},{2,3},{3,4},{4,5},{5,6},{6,7},{8,9},{9,10},{10,11},{11... | collective-permute-start | bytes 49160 | tf_op jit(solution)/shard_map/ppermute | solution.py:16
  215.4 1.3 collective-permute-start.15
  218.5 2.7 collective-permute-done.15
  222.6 6.5 %all_gather.47 = bf16[4,8,8192]{2,1,0:T(8,128)(2,1)S(1)} all-gather(bf16[1,8,8192]{2,1,0:T(8,128)(2,1)S(1)} %convert_element_type.244), channel_id=1, replica_groups=mesh['tm'=4,'space'=8] {'tm'}, dimensions={0}, use_global_device_ids=true | all-gather | bytes 655360 | tf_op jit(solution)/shard_map/all_gather | solution.py:149
  230.6 1.8 convolution_bitcast_fusion.2
  236.2 1.2 broadcast_multiply_fusion
  237.4 1.2 broadcast_multiply_fusion.1
  238.6 1.6 copy.155
  240.2 134.1 %all-reduce.38.cloned.1.call-done = (f32[4,3,3,64,64]{4,3,2,1,0:T(8,128)}, f32[4,3,3,64,64]{4,3,2,1,0:T(8,128)}) async-done(((f32[4,3,3,64,64]{4,3,2,1,0:T(8,128)}, f32[4,3,3,64,64]{4,3,2,1,0:T(8,128)}), (f32[4,3,3,64,64]{4,3,2,1,0:T(8,128)}, f32[4,3,3,64,64]{4,3,2,1,0:T(8,128)})) %all-reduce.38.cloned.1.call-update) | async-done | bytes 1179664 | tf_op jit(solution)/shard_map/psum | solution.py:175
  374.3 2.5 copy.332
  (337 shorter events, 64.5 us)
Async XLA Ops:
  7.2 70.9 %all-gather.4.cloned.1.call-start = ((), (), s32[]{:S(2)}) async-start(), calls=%async_computation | async-start | bytes 2621440 | tf_op jit(solution)/shard_map/all_gather | solution.py:149
  8.5 4.0 %copy-start.45 = (s32[4]{0:T(128)}, s32[4]{0:T(128)S(1)}, u32[]{:S(2)}) copy-start(s32[4]{0:T(128)S(1)} %get-tuple-element.44) | copy-start | bytes 52
  9.2 3.2 copy-start.41
  9.3 3.2 copy-start.43
  9.3 56.3 %copy-start.39 = (pred[4]{0:T(512)(128)(4,1)}, pred[4]{0:T(512)(128)(4,1)S(1)}, u32[]{:S(2)}) copy-start(pred[4]{0:T(512)(128)(4,1)S(1)} %get-tuple-element.149) | copy-start | bytes 16
  12.5 7.6 %copy-start.27 = (bf16[4,3,3,64,64]{4,3,2,1,0:T(8,128)(2,1)S(1)}, bf16[4,3,3,64,64]{4,3,2,1,0:T(8,128)(2,1)}, u32[]{:S(2)}) copy-start(bf16[4,3,3,64,64]{4,3,2,1,0:T(8,128)(2,1)} %param.11) | copy-start | bytes 884740
  13.1 12.7 %collective-permute-start = (bf16[4,1,8192]{2,0,1:T(4,128)(2,1)S(1)}, bf16[4,1,8192]{2,0,1:T(4,128)(2,1)S(1)}, u32[]{:S(2)}, u32[]{:S(2)}) collective-permute-start(bf16[4,1,8192]{2,0,1:T(4,128)(2,1)S(1)} %get-tuple-element.102), channel_id=1, source_target_pairs={{0,1},{1,2},{2,3},{3,4},{4,5},{5,6},{6,7},{8,9},{9,10},{10,11},{11... | collective-permute-start | bytes 196616 | tf_op jit(solution)/shard_map/ppermute | solution.py:16
  18.0 8.6 %collective-permute-start.1 = (bf16[4,1,8192]{2,0,1:T(4,128)(2,1)S(1)}, bf16[4,1,8192]{2,0,1:T(4,128)(2,1)S(1)}, u32[]{:S(2)}, u32[]{:S(2)}) collective-permute-start(bf16[4,1,8192]{2,0,1:T(4,128)(2,1)S(1)} %get-tuple-element.103), channel_id=1, source_target_pairs={{1,0},{2,1},{3,2},{4,3},{5,4},{6,5},{7,6},{9,8},{10,9},{11,10},{12... | collective-permute-start | bytes 196616 | tf_op jit(solution)/shard_map/ppermute | solution.py:18
  21.0 2.4 copy-start.28
  32.1 8.5 %copy-start.35 = (bf16[3,64,64]{2,1,0:T(8,128)(2,1)S(1)}, bf16[3,64,64]{2,1,0:T(8,128)(2,1)}, u32[]{:S(2)}) copy-start(bf16[3,64,64]{2,1,0:T(8,128)(2,1)} %get-tuple-element.135) | copy-start | bytes 73732
  32.1 8.5 %copy-start.36 = (bf16[3,64,64]{2,1,0:T(8,128)(2,1)S(1)}, bf16[3,64,64]{2,1,0:T(8,128)(2,1)}, u32[]{:S(2)}) copy-start(bf16[3,64,64]{2,1,0:T(8,128)(2,1)} %get-tuple-element.136) | copy-start | bytes 73732
  34.5 11.2 %copy-start = (bf16[4,8,8192]{2,0,1:T(4,128)(2,1)}, bf16[4,8,8192]{2,0,1:T(4,128)(2,1)S(1)}, u32[]{:S(2)}) copy-start(bf16[4,8,8192]{2,0,1:T(4,128)(2,1)S(1)} %fusion) | copy-start | bytes 1572868
  34.6 6.4 %collective-permute-start.2 = (bf16[4,1,8192]{2,0,1:T(4,128)(2,1)S(1)}, bf16[4,1,8192]{2,0,1:T(4,128)(2,1)S(1)}, u32[]{:S(2)}, u32[]{:S(2)}) collective-permute-start(bf16[4,1,8192]{2,0,1:T(4,128)(2,1)S(1)} %get-tuple-element.100), channel_id=1, source_target_pairs={{0,1},{1,2},{2,3},{3,4},{4,5},{5,6},{6,7},{8,9},{9,10},{10,11},{11... | collective-permute-start | bytes 196616 | tf_op jit(solution)/shard_map/ppermute | solution.py:16
  39.2 6.6 %collective-permute-start.3 = (bf16[4,1,8192]{2,0,1:T(4,128)(2,1)S(1)}, bf16[4,1,8192]{2,0,1:T(4,128)(2,1)S(1)}, u32[]{:S(2)}, u32[]{:S(2)}) collective-permute-start(bf16[4,1,8192]{2,0,1:T(4,128)(2,1)S(1)} %get-tuple-element.101), channel_id=1, source_target_pairs={{1,0},{2,1},{3,2},{4,3},{5,4},{6,5},{7,6},{9,8},{10,9},{11,10},{12... | collective-permute-start | bytes 196616 | tf_op jit(solution)/shard_map/ppermute | solution.py:18
  53.5 8.5 %copy-start.61 = (u32[32]{0:T(128)S(1)}, u32[32]{0:T(128)}, u32[]{:S(2)}) copy-start(u32[32]{0:T(128)} %constant.110) | copy-start | bytes 388
  53.5 10.6 %copy-start.25 = (bf16[1,3,3,64,64]{4,3,2,1,0:T(8,128)(2,1)S(1)}, bf16[1,3,3,64,64]{4,3,2,1,0:T(8,128)(2,1)}, u32[]{:S(2)}) copy-start(bf16[1,3,3,64,64]{4,3,2,1,0:T(8,128)(2,1)} %get-tuple-element.74) | copy-start | bytes 221188
  53.5 10.8 %copy-start.26 = (bf16[1,3,3,64,64]{4,3,2,1,0:T(8,128)(2,1)S(1)}, bf16[1,3,3,64,64]{4,3,2,1,0:T(8,128)(2,1)}, u32[]{:S(2)}) copy-start(bf16[1,3,3,64,64]{4,3,2,1,0:T(8,128)(2,1)} %get-tuple-element.70) | copy-start | bytes 221188
  53.5 10.9 %copy-start.56 = (s32[4]{0:T(128)S(1)}, s32[4]{0:T(128)}, u32[]{:S(2)}) copy-start(s32[4]{0:T(128)} %get-tuple-element.28) | copy-start | bytes 52
  53.5 11.2 %copy-start.55 = (s32[4]{0:T(128)S(1)}, s32[4]{0:T(128)}, u32[]{:S(2)}) copy-start(s32[4]{0:T(128)} %get-tuple-element.27) | copy-start | bytes 52
  53.5 11.4 %copy-start.54 = (s32[4]{0:T(128)S(1)}, s32[4]{0:T(128)}, u32[]{:S(2)}) copy-start(s32[4]{0:T(128)} %get-tuple-element.25) | copy-start | bytes 52
  53.6 11.6 %copy-start.53 = (s32[4]{0:T(128)S(1)}, s32[4]{0:T(128)}, u32[]{:S(2)}) copy-start(s32[4]{0:T(128)} %get-tuple-element.26) | copy-start | bytes 52
  53.6 11.8 %copy-start.52 = (s32[4,1]{0,1:T(1,128)S(1)}, s32[4,1]{0,1:T(1,128)}, u32[]{:S(2)}) copy-start(s32[4,1]{0,1:T(1,128)} %get-tuple-element.146) | copy-start | bytes 52
  53.6 21.1 %copy-start.51 = (s32[16,2]{0,1:T(2,128)S(1)}, s32[16,2]{0,1:T(2,128)}, u32[]{:S(2)}) copy-start(s32[16,2]{0,1:T(2,128)} %param.12) | copy-start | bytes 388
  53.6 88.8 %all-gather.6.cloned.1.call-start = ((), (), s32[]{:S(2)}) async-start(), calls=%async_computation.1 | async-start | bytes 2621440 | tf_op jit(solution)/shard_map/all_gather | solution.py:149
  55.1 23.0 %copy-start.31 = (bf16[4,8,8192]{2,1,0:T(8,128)(2,1)S(1)}, bf16[4,8,8192]{2,1,0:T(8,128)(2,1)}, u32[]{:S(2)}) copy-start(bf16[4,8,8192]{2,1,0:T(8,128)(2,1)} %param.7) | copy-start | bytes 1572868
  55.1 112.0 %collective-permute-start.16 = (bf16[2,4,1,8192]{3,2,1,0:T(2,128)(2,1)}, bf16[2,4,1,8192]{3,2,1,0:T(2,128)(2,1)}, u32[]{:S(2)}, u32[]{:S(2)}) collective-permute-start(bf16[2,4,1,8192]{3,2,1,0:T(2,128)(2,1)} %get-tuple-element.54), channel_id=1, source_target_pairs={{0,1},{1,2},{2,3},{3,4},{4,5},{5,6},{6,7},{8,9},{9,10},{10,11},{11... | collective-permute-start | bytes 393224 | tf_op jit(solution)/shard_map/ppermute | solution.py:16
  60.8 106.3 %collective-permute-start.17 = (bf16[2,4,1,8192]{3,2,1,0:T(2,128)(2,1)}, bf16[2,4,1,8192]{3,2,1,0:T(2,128)(2,1)}, u32[]{:S(2)}, u32[]{:S(2)}) collective-permute-start(bf16[2,4,1,8192]{3,2,1,0:T(2,128)(2,1)} %get-tuple-element.55), channel_id=1, source_target_pairs={{1,0},{2,1},{3,2},{4,3},{5,4},{6,5},{7,6},{9,8},{10,9},{11,10},{12... | collective-permute-start | bytes 393224 | tf_op jit(solution)/shard_map/ppermute | solution.py:18
  84.2 6.7 %collective-permute-start.4 = (bf16[4,1,8192]{2,0,1:T(4,128)(2,1)S(1)}, bf16[4,1,8192]{2,0,1:T(4,128)(2,1)S(1)}, u32[]{:S(2)}, u32[]{:S(2)}) collective-permute-start(bf16[4,1,8192]{2,0,1:T(4,128)(2,1)S(1)} %get-tuple-element.98), channel_id=1, source_target_pairs={{0,1},{1,2},{2,3},{3,4},{4,5},{5,6},{6,7},{8,9},{9,10},{10,11},{11... | collective-permute-start | bytes 196616 | tf_op jit(solution)/shard_map/ppermute | solution.py:16
  87.6 6.2 %collective-permute-start.5 = (bf16[4,1,8192]{2,0,1:T(4,128)(2,1)S(1)}, bf16[4,1,8192]{2,0,1:T(4,128)(2,1)S(1)}, u32[]{:S(2)}, u32[]{:S(2)}) collective-permute-start(bf16[4,1,8192]{2,0,1:T(4,128)(2,1)S(1)} %get-tuple-element.99), channel_id=1, source_target_pairs={{1,0},{2,1},{3,2},{4,3},{5,4},{6,5},{7,6},{9,8},{10,9},{11,10},{12... | collective-permute-start | bytes 196616 | tf_op jit(solution)/shard_map/ppermute | solution.py:18
  101.7 10.5 %copy-start.2 = (bf16[4,8,8192]{2,0,1:T(4,128)(2,1)}, bf16[4,8,8192]{2,0,1:T(4,128)(2,1)S(1)}, u32[]{:S(2)}) copy-start(bf16[4,8,8192]{2,0,1:T(4,128)(2,1)S(1)} %fusion.1) | copy-start | bytes 1572868
  101.7 6.2 %collective-permute-start.6 = (bf16[4,1,8192]{2,0,1:T(4,128)(2,1)S(1)}, bf16[4,1,8192]{2,0,1:T(4,128)(2,1)S(1)}, u32[]{:S(2)}, u32[]{:S(2)}) collective-permute-start(bf16[4,1,8192]{2,0,1:T(4,128)(2,1)S(1)} %get-tuple-element.96), channel_id=1, source_target_pairs={{0,1},{1,2},{2,3},{3,4},{4,5},{5,6},{6,7},{8,9},{9,10},{10,11},{11... | collective-permute-start | bytes 196616 | tf_op jit(solution)/shard_map/ppermute | solution.py:16
  106.0 6.2 %collective-permute-start.7 = (bf16[4,1,8192]{2,0,1:T(4,128)(2,1)S(1)}, bf16[4,1,8192]{2,0,1:T(4,128)(2,1)S(1)}, u32[]{:S(2)}, u32[]{:S(2)}) collective-permute-start(bf16[4,1,8192]{2,0,1:T(4,128)(2,1)S(1)} %get-tuple-element.97), channel_id=1, source_target_pairs={{1,0},{2,1},{3,2},{4,3},{5,4},{6,5},{7,6},{9,8},{10,9},{11,10},{12... | collective-permute-start | bytes 196616 | tf_op jit(solution)/shard_map/ppermute | solution.py:18
  119.5 1.6 copy-start.21
  119.5 1.8 copy-start.23
  120.5 72.2 %all-gather.8.cloned.1.call-start = ((), (), s32[]{:S(2)}) async-start(), calls=%async_computation.2 | async-start | bytes 1310720 | tf_op jit(solution)/shard_map/all_gather | solution.py:149
  122.3 2.0 copy-start.60
  122.3 2.0 copy-start.59
  122.3 2.0 copy-start.58
  122.3 2.5 copy-start.46
  122.3 2.6 copy-start.38
  122.6 19.9 %copy-start.14 = (f32[4,8,8192]{2,0,1:T(4,128)S(1)}, f32[4,8,8192]{2,0,1:T(4,128)}, u32[]{:S(2)}) copy-start(f32[4,8,8192]{2,0,1:T(4,128)} %get-tuple-element.153) | copy-start | bytes 3145732
  142.4 10.3 %copy-start.1 = (bf16[4,8,8192]{2,0,1:T(4,128)(2,1)S(1)}, bf16[4,8,8192]{2,0,1:T(4,128)(2,1)}, u32[]{:S(2)}) copy-start(bf16[4,8,8192]{2,0,1:T(4,128)(2,1)} %copy-done) | copy-start | bytes 1572868
  148.1 6.3 %collective-permute-start.8 = (bf16[2,1,8192]{2,0,1:T(2,128)(2,1)S(1)}, bf16[2,1,8192]{2,0,1:T(2,128)(2,1)S(1)}, u32[]{:S(2)}, u32[]{:S(2)}) collective-permute-start(bf16[2,1,8192]{2,0,1:T(2,128)(2,1)S(1)} %get-tuple-element.110), channel_id=1, source_target_pairs={{0,1},{1,2},{2,3},{3,4},{4,5},{5,6},{6,7},{8,9},{9,10},{10,11},{11... | collective-permute-start | bytes 98312 | tf_op jit(solution)/shard_map/ppermute | solution.py:16
  151.5 5.8 %collective-permute-start.9 = (bf16[2,1,8192]{2,0,1:T(2,128)(2,1)S(1)}, bf16[2,1,8192]{2,0,1:T(2,128)(2,1)S(1)}, u32[]{:S(2)}, u32[]{:S(2)}) collective-permute-start(bf16[2,1,8192]{2,0,1:T(2,128)(2,1)S(1)} %get-tuple-element.111), channel_id=1, source_target_pairs={{1,0},{2,1},{3,2},{4,3},{5,4},{6,5},{7,6},{9,8},{10,9},{11,10},{12... | collective-permute-start | bytes 98312 | tf_op jit(solution)/shard_map/ppermute | solution.py:18
  159.2 7.9 %copy-start.5 = (bf16[1,4,8,8192]{3,2,1,0:T(8,128)(2,1)S(1)}, bf16[1,4,8,8192]{3,2,1,0:T(8,128)(2,1)}, u32[]{:S(2)}) copy-start(bf16[1,4,8,8192]{3,2,1,0:T(8,128)(2,1)} %get-tuple-element.94) | copy-start | bytes 1572868
  159.2 7.9 %copy-start.9 = (bf16[4,8,8192]{2,1,0:T(8,128)(2,1)S(1)}, bf16[4,8,8192]{2,1,0:T(8,128)(2,1)}, u32[]{:S(2)}) copy-start(bf16[4,8,8192]{2,1,0:T(8,128)(2,1)} %param.8) | copy-start | bytes 1572868
  161.2 10.2 %copy-start.32 = (bf16[2,8,8192]{2,0,1:T(2,128)(2,1)}, bf16[2,8,8192]{2,0,1:T(2,128)(2,1)S(1)}, u32[]{:S(2)}) copy-start(bf16[2,8,8192]{2,0,1:T(2,128)(2,1)S(1)} %fusion.2) | copy-start | bytes 786436
  161.3 7.8 %collective-permute-start.10 = (bf16[2,1,8192]{2,0,1:T(2,128)(2,1)S(1)}, bf16[2,1,8192]{2,0,1:T(2,128)(2,1)S(1)}, u32[]{:S(2)}, u32[]{:S(2)}) collective-permute-start(bf16[2,1,8192]{2,0,1:T(2,128)(2,1)S(1)} %get-tuple-element.108), channel_id=1, source_target_pairs={{0,1},{1,2},{2,3},{3,4},{4,5},{5,6},{6,7},{8,9},{9,10},{10,11},{11... | collective-permute-start | bytes 98312 | tf_op jit(solution)/shard_map/ppermute | solution.py:16
  165.6 5.8 %collective-permute-start.11 = (bf16[2,1,8192]{2,0,1:T(2,128)(2,1)S(1)}, bf16[2,1,8192]{2,0,1:T(2,128)(2,1)S(1)}, u32[]{:S(2)}, u32[]{:S(2)}) collective-permute-start(bf16[2,1,8192]{2,0,1:T(2,128)(2,1)S(1)} %get-tuple-element.109), channel_id=1, source_target_pairs={{1,0},{2,1},{3,2},{4,3},{5,4},{6,5},{7,6},{9,8},{10,9},{11,10},{12... | collective-permute-start | bytes 98312 | tf_op jit(solution)/shard_map/ppermute | solution.py:18
  176.8 197.5 %all-reduce.38.cloned.1.call-start = ((), (), s32[]{:S(2)}) async-start(), calls=%async_computation.3 | async-start | bytes 4718592 | tf_op jit(solution)/shard_map/psum | solution.py:175
  188.9 3.8 copy-start.6
  195.4 5.5 %copy-start.33 = (bf16[2,8,8192]{2,0,1:T(2,128)(2,1)S(1)}, bf16[2,8,8192]{2,0,1:T(2,128)(2,1)}, u32[]{:S(2)}) copy-start(bf16[2,8,8192]{2,0,1:T(2,128)(2,1)} %copy-done.32) | copy-start | bytes 786436
  196.0 5.7 %collective-permute-start.12 = (bf16[1,1,8192]{2,1,0:T(2,128)(2,1)S(1)}, bf16[1,1,8192]{2,1,0:T(2,128)(2,1)S(1)}, u32[]{:S(2)}, u32[]{:S(2)}) collective-permute-start(bf16[1,1,8192]{2,1,0:T(2,128)(2,1)S(1)} %get-tuple-element.142), channel_id=1, source_target_pairs={{0,1},{1,2},{2,3},{3,4},{4,5},{5,6},{6,7},{8,9},{9,10},{10,11},{11... | collective-permute-start | bytes 49160 | tf_op jit(solution)/shard_map/ppermute | solution.py:16
  199.4 5.8 %collective-permute-start.13 = (bf16[1,1,8192]{2,1,0:T(2,128)(2,1)S(1)}, bf16[1,1,8192]{2,1,0:T(2,128)(2,1)S(1)}, u32[]{:S(2)}, u32[]{:S(2)}) collective-permute-start(bf16[1,1,8192]{2,1,0:T(2,128)(2,1)S(1)} %get-tuple-element.143), channel_id=1, source_target_pairs={{1,0},{2,1},{3,2},{4,3},{5,4},{6,5},{7,6},{9,8},{10,9},{11,10},{12... | collective-permute-start | bytes 49160 | tf_op jit(solution)/shard_map/ppermute | solution.py:18
  201.6 4.3 %copy-start.29 = (bf16[3,256,128]{2,1,0:T(8,128)(2,1)S(1)}, bf16[3,256,128]{2,1,0:T(8,128)(2,1)}, u32[]{:S(2)}) copy-start(bf16[3,256,128]{2,1,0:T(8,128)(2,1)} %fusion.118) | copy-start | bytes 589828
  211.1 7.2 %collective-permute-start.14 = (bf16[1,1,8192]{2,1,0:T(2,128)(2,1)S(1)}, bf16[1,1,8192]{2,1,0:T(2,128)(2,1)S(1)}, u32[]{:S(2)}, u32[]{:S(2)}) collective-permute-start(bf16[1,1,8192]{2,1,0:T(2,128)(2,1)S(1)} %get-tuple-element.140), channel_id=1, source_target_pairs={{0,1},{1,2},{2,3},{3,4},{4,5},{5,6},{6,7},{8,9},{9,10},{10,11},{11... | collective-permute-start | bytes 49160 | tf_op jit(solution)/shard_map/ppermute | solution.py:16
  215.4 5.8 %collective-permute-start.15 = (bf16[1,1,8192]{2,1,0:T(2,128)(2,1)S(1)}, bf16[1,1,8192]{2,1,0:T(2,128)(2,1)S(1)}, u32[]{:S(2)}, u32[]{:S(2)}) collective-permute-start(bf16[1,1,8192]{2,1,0:T(2,128)(2,1)S(1)} %get-tuple-element.141), channel_id=1, source_target_pairs={{1,0},{2,1},{3,2},{4,3},{5,4},{6,5},{7,6},{9,8},{10,9},{11,10},{12... | collective-permute-start | bytes 49160 | tf_op jit(solution)/shard_map/ppermute | solution.py:18
  218.0 3.7 copy-start.30
  222.0 7.1 %copy-start.49 = (s32[4]{0:T(128)S(1)}, s32[4]{0:T(128)}, u32[]{:S(2)}) copy-start(s32[4]{0:T(128)} %get-tuple-element.19) | copy-start | bytes 52
  222.0 7.1 %copy-start.50 = (s32[4]{0:T(128)S(1)}, s32[4]{0:T(128)}, u32[]{:S(2)}) copy-start(s32[4]{0:T(128)} %get-tuple-element.20) | copy-start | bytes 52
  222.0 7.1 %copy-start.57 = (f32[4]{0:T(128)S(1)}, f32[4]{0:T(128)}, u32[]{:S(2)}) copy-start(f32[4]{0:T(128)} %convert_multiply_fusion.2) | copy-start | bytes 52
  230.6 1.8 copy-start.17
  230.6 1.8 copy-start.18
  374.3 2.5 copy-start.12
  (20 other events, 21.7 us)
Sparse Core Ops, SparseCore 0:
  53.7 24.2 all-gather.3
  120.7 21.7 all-gather.5
  176.9 15.7 all-gather.7
  238.7 135.5 all-reduce.37
where the time goes:
time: 392 us; the launch traced here: 385 us
  waiting for transfers between devices  178 us (45%)
  local copies, waits for them, and re-layouts  60 us (15%)
  starting transfers between devices  51.1 us (13%)
  matrix products  39.3 us (10%)
  other arithmetic  27.3 us (7%)
  between operations  17.3 us (4%)
  blocking collectives  12.2 us (3%)
    psum x1, waiting for transfers between devices, body_time(): weight_one, weight_two = lax.psum((sum_one, sum_two), ('tm', 'space'))  134 us
    ppermute x9, starting transfers between devices, padded_2(): lax.ppermute(tail, axis, [(i, (i + 1) % count) for i in range(ends)])  38.1 us
    ppermute x9, waiting for transfers between devices, padded_2(): lax.ppermute(head, axis, [((i + 1) % count, i) for i in range(ends)])  21.9 us
    all_gather x3, waiting for transfers between devices, body_time(): moved = lax.all_gather(to_refs, 'tm', axis=0, tiled=True)  20.7 us
    unnamed x158, local copies, waits for them, and re-layouts  18.8 us
    dot_general x4, matrix products, body_time(): jnp.einsum('kf,kx->fx', weights.astype(jnp.bfloat16), moved.reshape(moved...  14.4 us
    ppermute x9, starting transfers between devices, padded_2(): lax.ppermute(head, axis, [((i + 1) % count, i) for i in range(ends)])  12.7 us
    dot_general x4, matrix products, body_time(): jnp.einsum('sf,fx->sx', picker_wide, act_slope.reshape(frames_dev, -1), p...  9.11 us
  transfers between devices with their start and end apart: 22, of which 13 were waited for; matrix products, arithmetic and copies ran while one was open for 19% of the time, Pallas kernels for 0%

commit v1 on v0

--- a/solution.py
+++ b/solution.py
@@ -146,7 +146,25 @@
         )
         frame_grad = frame_grad.astype(jnp.bfloat16).reshape(kept_grad.shape)
         kept_grad = jnp.where(active[:, None, None], frame_grad, kept_grad)
-        moved = lax.all_gather(to_refs, "tm", axis=0, tiled=True)
+        ways, here, turn = (lax.axis_size("tm"), lax.axis_index("tm"), to_refs.shape[0])
+        lengths = [n * ways if d == 0 else n for d, n in enumerate(to_refs.shape)]
+        full = lax.dynamic_update_slice_in_dim(
+            jnp.zeros(lengths, to_refs.dtype), to_refs, here * turn, axis=0
+        )
+        going_up = going_down = to_refs
+        for far in range(1, ways // 2 + 1):
+            going_up = lax.ppermute(going_up, "tm", [(d, (d + 1) % ways) for d in range(ways)])
+            full = lax.dynamic_update_slice_in_dim(
+                full, going_up, (here - far) % ways * turn, axis=0
+            )
+            if 2 * far < ways:
+                going_down = lax.ppermute(
+                    going_down, "tm", [(d, (d - 1) % ways) for d in range(ways)]
+                )
+                full = lax.dynamic_update_slice_in_dim(
+                    full, going_down, (here + far) % ways * turn, axis=0
+                )
+        moved = full
         sender_ids = lax.all_gather(slot_ids, "tm", axis=0, tiled=True)
         sender_ok = lax.all_gather(slot_ok, "tm", axis=0, tiled=True)
         matches = (sender_ids[:, None] == all_frames[None, :]).astype(jnp.int32)

time: 392 us -> 438 us (1.12)
  starting transfers between devices: 51.1 us -> 70.5 us
  waiting for transfers between devices: 178 us -> 196 us
  other arithmetic: 27.3 us -> 38 us
  local copies, waits for them, and re-layouts: 60 us -> 68 us
  blocking collectives: 12.2 us -> 5.88 us
    ppermute x0 -> x12, waiting for transfers between devices: none -> 56.8 us  [the longest x8 56.4 us: body_time(): lax.ppermute(going_up, 'tm', [(d, (d + 1) % ways) for d in range(ways)])]
    ppermute x9, waiting for transfers between devices: 21.9 us -> 0.02 us  [padded_2(): lax.ppermute(head, axis, [((i + 1) % count, i) for i in range(ends)])]
    all_gather x3 -> x0, waiting for transfers between devices: 20.7 us -> none  [body_time(): moved = lax.all_gather(to_refs, 'tm', axis=0, tiled=True)]
    ppermute x9, starting transfers between devices: 38.1 us -> 51.5 us  [padded_2(): lax.ppermute(tail, axis, [(i, (i + 1) % count) for i in range(ends)])]
    ppermute x0 -> x12, starting transfers between devices: none -> 7.17 us  [the longest x4 6.93 us: body_time(): lax.ppermute(going_down, 'tm', [(d, (d - 1) % ways) for d in range(ways)])]
    all_gather x1 -> x0, blocking collectives: 6.5 us -> none  [body_time(): moved = lax.all_gather(to_refs, 'tm', axis=0, tiled=True)]
    dot_general x4, matrix products: 14.4 us -> 8.94 us  [body_time(): jnp.einsum('kf,kx->fx', weights.astype(jnp.bfloat16), moved.reshape(moved...]
    unnamed x158 -> x144, local copies, waits for them, and re-layouts: 18.8 us -> 20.6 us
  transfers between devices with their start and end apart: 22 -> 31, of which waited for: 13 -> 13; matrix products, arithmetic and copies ran while one was open for 19% -> 17% of each run, Pallas kernels for 0% -> 0%
where the time goes in v1:
time: 438 us; the launch traced here: 432 us
  waiting for transfers between devices  196 us (45%)
  starting transfers between devices  70.5 us (16%)
  local copies, waits for them, and re-layouts  68 us (16%)
  other arithmetic  38 us (9%)
  matrix products  36.2 us (8%)
  between operations  17.6 us (4%)
  blocking collectives  5.88 us (1%)
    psum x1, waiting for transfers between devices, body_time(): weight_one, weight_two = lax.psum((sum_one, sum_two), ('tm', 'space'))  138 us
    ppermute x8, waiting for transfers between devices, body_time(): lax.ppermute(going_up, 'tm', [(d, (d + 1) % ways) for d in range(ways)])  56.4 us
    ppermute x9, starting transfers between devices, padded_2(): lax.ppermute(tail, axis, [(i, (i + 1) % count) for i in range(ends)])  51.5 us
    unnamed x144, local copies, waits for them, and re-layouts  20.6 us
    ppermute x9, starting transfers between devices, padded_2(): lax.ppermute(head, axis, [((i + 1) % count, i) for i in range(ends)])  11.7 us
    dot_general x4, matrix products, body_time(): jnp.einsum('sf,fx->sx', picker_wide, act_slope.reshape(frames_dev, -1), p...  11.3 us
    concatenate x9, other arithmetic, padded_2(): jnp.concatenate([lax.ppermute(tail, axis, [(i, (i + 1) % count) for i in...  9.74 us
    reshape x10, local copies, waits for them, and re-layouts, pair_view(): grid.reshape(field.shape[0], field.shape[1], (col_count + 2) // 2, 2 * ch...  9.61 us
  transfers between devices with their start and end apart: 31, of which 13 were waited for; matrix products, arithmetic and copies ran while one was open for 17% of the time, Pallas kernels for 0%

profile of v1, /device:TPU:0, one launch (start us, length us, event | category | flops | bytes accessed | tf_op | source)
XLA Modules:
  0.0 431.9 jit_solution(9265403373183365008)
XLA Ops:
  7.2 1.3 broadcast_compare_fusion
  10.0 1.4 copy.174
  14.4 6.2 %collective-permute-start = (bf16[4,1,8192]{2,0,1:T(4,128)(2,1)}, bf16[4,1,8192]{2,0,1:T(4,128)(2,1)}, u32[]{:S(2)}, u32[]{:S(2)}) collective-permute-start(bf16[4,1,8192]{2,0,1:T(4,128)(2,1)} %get-tuple-element.99), channel_id=1, source_target_pairs={{0,1},{1,2},{2,3},{3,4},{4,5},{5,6},{6,7},{8,9},{9,10},{10,11},{11... | collective-permute-start | bytes 196616 | tf_op jit(solution)/shard_map/ppermute | solution.py:16
  23.1 1.3 collective-permute-start.29
  24.4 5.6 %collective-permute-start.28 = (bf16[2,4,1,8192]{3,2,1,0:T(2,128)(2,1)}, bf16[2,4,1,8192]{3,2,1,0:T(2,128)(2,1)}, u32[]{:S(2)}, u32[]{:S(2)}) collective-permute-start(bf16[2,4,1,8192]{3,2,1,0:T(2,128)(2,1)} %get-tuple-element.51), channel_id=1, source_target_pairs={{0,1},{1,2},{2,3},{3,4},{4,5},{5,6},{6,7},{8,9},{9,10},{10,11},{11... | collective-permute-start | bytes 393224 | tf_op jit(solution)/shard_map/ppermute | solution.py:16
  35.2 1.3 dynamic-update-slice.7
  37.8 5.9 %all-reduce.34 = (s32[16]{0:T(128)}, s32[16]{0:T(128)}, s32[16]{0:T(128)S(1)}, s32[16]{0:T(128)S(1)}, s32[8]{0:T(128)}, /*index=5*/s32[8]{0:T(128)}, s32[4]{0:T(128)S(1)}, s32[4]{0:T(128)}) all-reduce(s32[16]{0:T(128)S(1)} %dynamic-update-slice.3, s32[16]{0:T(128)S(1)} %dynamic-update-slice.1, ...), channel_id=1, replica_groups=mesh['tm'=4,'space'=8] {'tm'}, use_global_device_ids=true, to_apply=%add.29 | all-reduce | flops 88 | bytes 704
  50.1 2.4 fusion.143
  53.5 1.5 select_reduce_fusion.5
  55.0 1.4 select_reduce_fusion.1
  63.4 1.7 concatenate.214
  65.1 1.7 concatenate.212
  66.7 1.4 select_maximum_fusion.2
  71.5 2.4 fusion
  73.9 1.3 collective-permute-start.3
  75.2 4.8 %collective-permute-start.2 = (bf16[4,1,8192]{2,0,1:T(4,128)(2,1)S(1)}, bf16[4,1,8192]{2,0,1:T(4,128)(2,1)S(1)}, u32[]{:S(2)}, u32[]{:S(2)}) collective-permute-start(bf16[4,1,8192]{2,0,1:T(4,128)(2,1)S(1)} %get-tuple-element.97), channel_id=1, source_target_pairs={{0,1},{1,2},{2,3},{3,4},{4,5},{5,6},{6,7},{8,9},{9,10},{10,11},{11... | collective-permute-start | bytes 196616 | tf_op jit(solution)/shard_map/ppermute | solution.py:16
  82.2 1.9 reshape.439
  84.1 1.8 pad.50
  89.3 1.7 collective-permute-start.5
  91.1 2.0 pad_maximum_fusion
  93.3 9.0 %collective-permute-done.4 = bf16[4,8,8192]{2,1,0:T(8,128)(2,1)S(1)} collective-permute-done((bf16[4,8,8192]{2,1,0:T(8,128)(2,1)S(1)}, bf16[4,8,8192]{2,1,0:T(8,128)(2,1)S(1)}, u32[]{:S(2)}, u32[]{:S(2)}) %collective-permute-start.4) | collective-permute-done | bytes 524320 | tf_op jit(solution)/shard_map/ppermute | solution.py:156
  102.5 8.5 %collective-permute-done.6 = bf16[4,8,8192]{2,1,0:T(8,128)(2,1)S(1)} collective-permute-done((bf16[4,8,8192]{2,1,0:T(8,128)(2,1)S(1)}, bf16[4,8,8192]{2,1,0:T(8,128)(2,1)S(1)}, u32[]{:S(2)}, u32[]{:S(2)}) %collective-permute-start.6) | collective-permute-done | bytes 524320 | tf_op jit(solution)/shard_map/ppermute | solution.py:156
  111.0 4.0 fusion.214
  115.6 1.3 collective-permute-start.8
  116.9 5.9 %collective-permute-start.7 = (bf16[4,1,8192]{2,0,1:T(4,128)(2,1)S(1)}, bf16[4,1,8192]{2,0,1:T(4,128)(2,1)S(1)}, u32[]{:S(2)}, u32[]{:S(2)}) collective-permute-start(bf16[4,1,8192]{2,0,1:T(4,128)(2,1)S(1)} %get-tuple-element.95), channel_id=1, source_target_pairs={{0,1},{1,2},{2,3},{3,4},{4,5},{5,6},{6,7},{8,9},{9,10},{10,11},{11... | collective-permute-start | bytes 196616 | tf_op jit(solution)/shard_map/ppermute | solution.py:16
  124.4 1.9 reshape_squeeze.6
  126.3 1.8 pad.57
  129.0 1.9 concatenate.230
  131.3 1.6 select_maximum_fusion
  132.9 1.9 reshape.445
  138.2 3.6 fusion.1
  142.6 1.4 collective-permute-start.10
  144.0 6.0 %collective-permute-start.9 = (bf16[4,1,8192]{2,0,1:T(4,128)(2,1)S(1)}, bf16[4,1,8192]{2,0,1:T(4,128)(2,1)S(1)}, u32[]{:S(2)}, u32[]{:S(2)}) collective-permute-start(bf16[4,1,8192]{2,0,1:T(4,128)(2,1)S(1)} %get-tuple-element.93), channel_id=1, source_target_pairs={{0,1},{1,2},{2,3},{3,4},{4,5},{5,6},{6,7},{8,9},{9,10},{10,11},{11... | collective-permute-start | bytes 196616 | tf_op jit(solution)/shard_map/ppermute | solution.py:16
  150.0 1.3 fusion.194
  151.8 1.9 reshape_squeeze.7
  153.8 1.8 pad.58
  156.4 2.4 pad_maximum_fusion.10
  158.8 2.1 reshape.447
  160.9 1.6 pad.52
  162.5 1.9 reshape.569
  166.9 1.7 collective-permute-start.12
  169.0 11.3 %collective-permute-done.11 = bf16[4,8,8192]{2,1,0:T(8,128)(2,1)S(1)} collective-permute-done((bf16[4,8,8192]{2,1,0:T(8,128)(2,1)S(1)}, bf16[4,8,8192]{2,1,0:T(8,128)(2,1)S(1)}, u32[]{:S(2)}, u32[]{:S(2)}) %collective-permute-start.11) | collective-permute-done | bytes 524320 | tf_op jit(solution)/shard_map/ppermute | solution.py:156
  180.4 8.5 %collective-permute-done.13 = bf16[4,8,8192]{2,1,0:T(8,128)(2,1)S(1)} collective-permute-done((bf16[4,8,8192]{2,1,0:T(8,128)(2,1)S(1)}, bf16[4,8,8192]{2,1,0:T(8,128)(2,1)S(1)}, u32[]{:S(2)}, u32[]{:S(2)}) %collective-permute-start.13) | collective-permute-done | bytes 524320 | tf_op jit(solution)/shard_map/ppermute | solution.py:156
  189.0 2.5 fusion.215
  192.0 1.3 collective-permute-start.15
  193.3 5.6 %collective-permute-start.14 = (bf16[2,1,8192]{2,0,1:T(2,128)(2,1)S(1)}, bf16[2,1,8192]{2,0,1:T(2,128)(2,1)S(1)}, u32[]{:S(2)}, u32[]{:S(2)}) collective-permute-start(bf16[2,1,8192]{2,0,1:T(2,128)(2,1)S(1)} %get-tuple-element.107), channel_id=1, source_target_pairs={{0,1},{1,2},{2,3},{3,4},{4,5},{5,6},{6,7},{8,9},{9,10},{10,11},{11... | collective-permute-start | bytes 98312 | tf_op jit(solution)/shard_map/ppermute | solution.py:16
  201.9 1.5 reshape.453
  205.5 3.0 fusion.2
  208.5 1.3 collective-permute-start.17
  209.8 5.4 %collective-permute-start.16 = (bf16[2,1,8192]{2,0,1:T(2,128)(2,1)S(1)}, bf16[2,1,8192]{2,0,1:T(2,128)(2,1)S(1)}, u32[]{:S(2)}, u32[]{:S(2)}) collective-permute-start(bf16[2,1,8192]{2,0,1:T(2,128)(2,1)S(1)} %get-tuple-element.105), channel_id=1, source_target_pairs={{0,1},{1,2},{2,3},{3,4},{4,5},{5,6},{6,7},{8,9},{9,10},{10,11},{11... | collective-permute-start | bytes 98312 | tf_op jit(solution)/shard_map/ppermute | solution.py:16
  220.1 1.7 collective-permute-start.19
  221.9 6.7 %collective-permute-done.18 = bf16[2,8,8192]{2,1,0:T(8,128)(2,1)S(1)} collective-permute-done((bf16[2,8,8192]{2,1,0:T(8,128)(2,1)S(1)}, bf16[2,8,8192]{2,1,0:T(8,128)(2,1)S(1)}, u32[]{:S(2)}, u32[]{:S(2)}) %collective-permute-start.18) | collective-permute-done | bytes 262176 | tf_op jit(solution)/shard_map/ppermute | solution.py:156
  228.7 5.7 %collective-permute-done.20 = bf16[2,8,8192]{2,1,0:T(8,128)(2,1)S(1)} collective-permute-done((bf16[2,8,8192]{2,1,0:T(8,128)(2,1)S(1)}, bf16[2,8,8192]{2,1,0:T(8,128)(2,1)S(1)}, u32[]{:S(2)}, u32[]{:S(2)}) %collective-permute-start.20) | collective-permute-done | bytes 262176 | tf_op jit(solution)/shard_map/ppermute | solution.py:156
  234.5 1.5 fusion.216
  236.5 1.3 collective-permute-start.22
  237.8 5.7 %collective-permute-start.21 = (bf16[1,1,8192]{2,1,0:T(2,128)(2,1)S(1)}, bf16[1,1,8192]{2,1,0:T(2,128)(2,1)S(1)}, u32[]{:S(2)}, u32[]{:S(2)}) collective-permute-start(bf16[1,1,8192]{2,1,0:T(2,128)(2,1)S(1)} %get-tuple-element.139), channel_id=1, source_target_pairs={{0,1},{1,2},{2,3},{3,4},{4,5},{5,6},{6,7},{8,9},{9,10},{10,11},{11... | collective-permute-start | bytes 49160 | tf_op jit(solution)/shard_map/ppermute | solution.py:16
  252.1 6.4 %collective-permute-start.23 = (bf16[1,1,8192]{2,1,0:T(2,128)(2,1)}, bf16[1,1,8192]{2,1,0:T(2,128)(2,1)}, u32[]{:S(2)}, u32[]{:S(2)}) collective-permute-start(bf16[1,1,8192]{2,1,0:T(2,128)(2,1)} %get-tuple-element.137), channel_id=1, source_target_pairs={{0,1},{1,2},{2,3},{3,4},{4,5},{5,6},{6,7},{8,9},{9,10},{10,11},{11... | collective-permute-start | bytes 49160 | tf_op jit(solution)/shard_map/ppermute | solution.py:16
  263.3 1.7 collective-permute-start.26
  265.1 2.6 collective-permute-done.25
  268.1 4.0 collective-permute-done.27
  273.7 1.8 convolution_bitcast_fusion
  281.6 1.6 copy.114
  283.2 137.9 %all-reduce.38.cloned.1.call-done = (f32[4,3,3,64,64]{4,3,2,1,0:T(8,128)}, f32[4,3,3,64,64]{4,3,2,1,0:T(8,128)}) async-done(((f32[4,3,3,64,64]{4,3,2,1,0:T(8,128)}, f32[4,3,3,64,64]{4,3,2,1,0:T(8,128)}), (f32[4,3,3,64,64]{4,3,2,1,0:T(8,128)}, f32[4,3,3,64,64]{4,3,2,1,0:T(8,128)})) %all-reduce.38.cloned.1.call-update) | async-done | bytes 1179664 | tf_op jit(solution)/shard_map/psum | solution.py:193
  421.1 2.5 copy.332
  (357 shorter events, 80.4 us)
Async XLA Ops:
  7.2 13.4 %copy-start.25 = (bf16[4,8,8192]{2,1,0:T(8,128)(2,1)S(1)}, bf16[4,8,8192]{2,1,0:T(8,128)(2,1)}, u32[]{:S(2)}) copy-start(bf16[4,8,8192]{2,1,0:T(8,128)(2,1)} %param.9) | copy-start | bytes 1572868
  7.2 413.9 %all-reduce.38.cloned.1.call-start = ((), (), s32[]{:S(2)}) async-start(), calls=%async_computation | async-start | bytes 4718592 | tf_op jit(solution)/shard_map/psum | solution.py:193
  9.3 11.7 %copy-start.34 = (pred[4]{0:T(512)(128)(4,1)}, pred[4]{0:T(512)(128)(4,1)S(1)}, u32[]{:S(2)}) copy-start(pred[4]{0:T(512)(128)(4,1)S(1)} %get-tuple-element.147) | copy-start | bytes 16
  9.3 11.8 %copy-start.36 = (pred[4]{0:T(512)(128)(4,1)}, pred[4]{0:T(512)(128)(4,1)S(1)}, u32[]{:S(2)}) copy-start(pred[4]{0:T(512)(128)(4,1)S(1)} %get-tuple-element.148) | copy-start | bytes 16
  9.3 24.8 %copy-start.32 = (pred[4]{0:T(512)(128)(4,1)}, pred[4]{0:T(512)(128)(4,1)S(1)}, u32[]{:S(2)}) copy-start(pred[4]{0:T(512)(128)(4,1)S(1)} %get-tuple-element.146) | copy-start | bytes 16
  9.3 40.8 %copy-start.30 = (pred[4]{0:T(512)(128)(4,1)}, pred[4]{0:T(512)(128)(4,1)S(1)}, u32[]{:S(2)}) copy-start(pred[4]{0:T(512)(128)(4,1)S(1)} %get-tuple-element.43) | copy-start | bytes 16
  12.4 9.4 %copy-start.6 = (bf16[4,8,8192]{2,1,0:T(8,128)(2,1)S(1)}, bf16[4,8,8192]{2,1,0:T(8,128)(2,1)}, u32[]{:S(2)}) copy-start(bf16[4,8,8192]{2,1,0:T(8,128)(2,1)} %param.8) | copy-start | bytes 1572868
  13.1 50.3 %collective-permute-start.1 = (bf16[4,1,8192]{2,0,1:T(4,128)(2,1)}, bf16[4,1,8192]{2,0,1:T(4,128)(2,1)}, u32[]{:S(2)}, u32[]{:S(2)}) collective-permute-start(bf16[4,1,8192]{2,0,1:T(4,128)(2,1)} %get-tuple-element.100), channel_id=1, source_target_pairs={{1,0},{2,1},{3,2},{4,3},{5,4},{6,5},{7,6},{9,8},{10,9},{11,10},{12... | collective-permute-start | bytes 196616 | tf_op jit(solution)/shard_map/ppermute | solution.py:18
  14.4 50.6 %collective-permute-start = (bf16[4,1,8192]{2,0,1:T(4,128)(2,1)}, bf16[4,1,8192]{2,0,1:T(4,128)(2,1)}, u32[]{:S(2)}, u32[]{:S(2)}) collective-permute-start(bf16[4,1,8192]{2,0,1:T(4,128)(2,1)} %get-tuple-element.99), channel_id=1, source_target_pairs={{0,1},{1,2},{2,3},{3,4},{4,5},{5,6},{6,7},{8,9},{9,10},{10,11},{11... | collective-permute-start | bytes 196616 | tf_op jit(solution)/shard_map/ppermute | solution.py:16
  21.8 9.7 %copy-start.53 = (u32[32]{0:T(128)S(1)}, u32[32]{0:T(128)}, u32[]{:S(2)}) copy-start(u32[32]{0:T(128)} %constant.154) | copy-start | bytes 388
  21.8 11.4 %copy-start.46 = (s32[16,2]{0,1:T(2,128)S(1)}, s32[16,2]{0,1:T(2,128)}, u32[]{:S(2)}) copy-start(s32[16,2]{0,1:T(2,128)} %param.12) | copy-start | bytes 388
  21.8 22.4 %copy-start.21 = (bf16[4,3,3,64,64]{4,3,2,1,0:T(8,128)(2,1)S(1)}, bf16[4,3,3,64,64]{4,3,2,1,0:T(8,128)(2,1)}, u32[]{:S(2)}) copy-start(bf16[4,3,3,64,64]{4,3,2,1,0:T(8,128)(2,1)} %param.10) | copy-start | bytes 884740
  23.1 68.0 %collective-permute-start.29 = (bf16[2,4,1,8192]{3,2,1,0:T(2,128)(2,1)}, bf16[2,4,1,8192]{3,2,1,0:T(2,128)(2,1)}, u32[]{:S(2)}, u32[]{:S(2)}) collective-permute-start(bf16[2,4,1,8192]{3,2,1,0:T(2,128)(2,1)} %get-tuple-element.52), channel_id=1, source_target_pairs={{1,0},{2,1},{3,2},{4,3},{5,4},{6,5},{7,6},{9,8},{10,9},{11,10},{12... | collective-permute-start | bytes 393224 | tf_op jit(solution)/shard_map/ppermute | solution.py:18
  24.4 66.7 %collective-permute-start.28 = (bf16[2,4,1,8192]{3,2,1,0:T(2,128)(2,1)}, bf16[2,4,1,8192]{3,2,1,0:T(2,128)(2,1)}, u32[]{:S(2)}, u32[]{:S(2)}) collective-permute-start(bf16[2,4,1,8192]{3,2,1,0:T(2,128)(2,1)} %get-tuple-element.51), channel_id=1, source_target_pairs={{0,1},{1,2},{2,3},{3,4},{4,5},{5,6},{6,7},{8,9},{9,10},{10,11},{11... | collective-permute-start | bytes 393224 | tf_op jit(solution)/shard_map/ppermute | solution.py:16
  52.4 5.5 %copy-start.29 = (bf16[3,64,64]{2,1,0:T(8,128)(2,1)S(1)}, bf16[3,64,64]{2,1,0:T(8,128)(2,1)}, u32[]{:S(2)}) copy-start(bf16[3,64,64]{2,1,0:T(8,128)(2,1)} %get-tuple-element.127) | copy-start | bytes 73732
  73.9 7.4 %collective-permute-start.3 = (bf16[4,1,8192]{2,0,1:T(4,128)(2,1)S(1)}, bf16[4,1,8192]{2,0,1:T(4,128)(2,1)S(1)}, u32[]{:S(2)}, u32[]{:S(2)}) collective-permute-start(bf16[4,1,8192]{2,0,1:T(4,128)(2,1)S(1)} %get-tuple-element.98), channel_id=1, source_target_pairs={{1,0},{2,1},{3,2},{4,3},{5,4},{6,5},{7,6},{9,8},{10,9},{11,10},{12... | collective-permute-start | bytes 196616 | tf_op jit(solution)/shard_map/ppermute | solution.py:18
  75.2 6.5 %collective-permute-start.2 = (bf16[4,1,8192]{2,0,1:T(4,128)(2,1)S(1)}, bf16[4,1,8192]{2,0,1:T(4,128)(2,1)S(1)}, u32[]{:S(2)}, u32[]{:S(2)}) collective-permute-start(bf16[4,1,8192]{2,0,1:T(4,128)(2,1)S(1)} %get-tuple-element.97), channel_id=1, source_target_pairs={{0,1},{1,2},{2,3},{3,4},{4,5},{5,6},{6,7},{8,9},{9,10},{10,11},{11... | collective-permute-start | bytes 196616 | tf_op jit(solution)/shard_map/ppermute | solution.py:16
  88.5 2.5 copy-start.3
  88.5 2.5 copy-start.7
  89.2 13.1 %collective-permute-start.4 = (bf16[4,8,8192]{2,1,0:T(8,128)(2,1)S(1)}, bf16[4,8,8192]{2,1,0:T(8,128)(2,1)S(1)}, u32[]{:S(2)}, u32[]{:S(2)}) collective-permute-start(bf16[4,8,8192]{2,1,0:T(8,128)(2,1)S(1)} %convert_element_type.213), channel_id=1, source_target_pairs={{0,8},{8,16},{16,24},{24,0},{1,9},{9,17},{17,25},{25,1},{2,10},{10... | collective-permute-start | bytes 1572872 | tf_op jit(solution)/shard_map/ppermute | solution.py:156
  89.3 13.1 %collective-permute-start.5 = (bf16[4,8,8192]{2,1,0:T(8,128)(2,1)S(1)}, bf16[4,8,8192]{2,1,0:T(8,128)(2,1)S(1)}, u32[]{:S(2)}, u32[]{:S(2)}) collective-permute-start(bf16[4,8,8192]{2,1,0:T(8,128)(2,1)S(1)} %convert_element_type.213), channel_id=1, source_target_pairs={{0,24},{8,0},{16,8},{24,16},{1,25},{9,1},{17,9},{25,17},{2,26},{10... | collective-permute-start | bytes 1572872 | tf_op jit(solution)/shard_map/ppermute | solution.py:161
  93.3 17.7 %copy-start.24 = (bf16[4,8,8192]{2,1,0:T(8,128)(2,1)S(1)}, bf16[4,8,8192]{2,1,0:T(8,128)(2,1)}, u32[]{:S(2)}) copy-start(bf16[4,8,8192]{2,1,0:T(8,128)(2,1)} %param.7) | copy-start | bytes 1572868
  93.3 17.7 %copy-start.50 = (s32[16]{0:T(128)S(1)}, s32[16]{0:T(128)}, u32[]{:S(2)}) copy-start(s32[16]{0:T(128)} %get-tuple-element.27) | copy-start | bytes 196
  93.3 17.7 %copy-start.51 = (s32[16]{0:T(128)S(1)}, s32[16]{0:T(128)}, u32[]{:S(2)}) copy-start(s32[16]{0:T(128)} %get-tuple-element.28) | copy-start | bytes 196
  93.3 17.7 %copy-start.54 = (f32[16]{0:T(128)S(1)}, f32[16]{0:T(128)}, u32[]{:S(2)}) copy-start(f32[16]{0:T(128)} %convert_multiply_fusion.5) | copy-start | bytes 196
  102.4 8.6 %collective-permute-start.6 = (bf16[4,8,8192]{2,1,0:T(8,128)(2,1)S(1)}, bf16[4,8,8192]{2,1,0:T(8,128)(2,1)S(1)}, u32[]{:S(2)}, u32[]{:S(2)}) collective-permute-start(bf16[4,8,8192]{2,1,0:T(8,128)(2,1)S(1)} %collective-permute-done.4), channel_id=1, source_target_pairs={{0,8},{8,16},{16,24},{24,0},{1,9},{9,17},{17,25},{25,1},{2,10},{10... | collective-permute-start | bytes 1572872 | tf_op jit(solution)/shard_map/ppermute | solution.py:156
  115.6 15.3 %collective-permute-start.8 = (bf16[4,1,8192]{2,0,1:T(4,128)(2,1)S(1)}, bf16[4,1,8192]{2,0,1:T(4,128)(2,1)S(1)}, u32[]{:S(2)}, u32[]{:S(2)}) collective-permute-start(bf16[4,1,8192]{2,0,1:T(4,128)(2,1)S(1)} %get-tuple-element.96), channel_id=1, source_target_pairs={{1,0},{2,1},{3,2},{4,3},{5,4},{6,5},{7,6},{9,8},{10,9},{11,10},{12... | collective-permute-start | bytes 196616 | tf_op jit(solution)/shard_map/ppermute | solution.py:18
  116.9 14.2 %collective-permute-start.7 = (bf16[4,1,8192]{2,0,1:T(4,128)(2,1)S(1)}, bf16[4,1,8192]{2,0,1:T(4,128)(2,1)S(1)}, u32[]{:S(2)}, u32[]{:S(2)}) collective-permute-start(bf16[4,1,8192]{2,0,1:T(4,128)(2,1)S(1)} %get-tuple-element.95), channel_id=1, source_target_pairs={{0,1},{1,2},{2,3},{3,4},{4,5},{5,6},{6,7},{8,9},{9,10},{10,11},{11... | collective-permute-start | bytes 196616 | tf_op jit(solution)/shard_map/ppermute | solution.py:16
  142.6 8.8 %copy-start.4 = (bf16[1,4,10,8192]{3,2,1,0:T(8,128)(2,1)S(1)}, bf16[1,4,10,8192]{3,2,1,0:T(8,128)(2,1)}, u32[]{:S(2)}) copy-start(bf16[1,4,10,8192]{3,2,1,0:T(8,128)(2,1)} %get-tuple-element.50) | copy-start | bytes 1966084
  142.6 13.8 %collective-permute-start.10 = (bf16[4,1,8192]{2,0,1:T(4,128)(2,1)S(1)}, bf16[4,1,8192]{2,0,1:T(4,128)(2,1)S(1)}, u32[]{:S(2)}, u32[]{:S(2)}) collective-permute-start(bf16[4,1,8192]{2,0,1:T(4,128)(2,1)S(1)} %get-tuple-element.94), channel_id=1, source_target_pairs={{1,0},{2,1},{3,2},{4,3},{5,4},{6,5},{7,6},{9,8},{10,9},{11,10},{12... | collective-permute-start | bytes 196616 | tf_op jit(solution)/shard_map/ppermute | solution.py:18
  144.0 12.4 %collective-permute-start.9 = (bf16[4,1,8192]{2,0,1:T(4,128)(2,1)S(1)}, bf16[4,1,8192]{2,0,1:T(4,128)(2,1)S(1)}, u32[]{:S(2)}, u32[]{:S(2)}) collective-permute-start(bf16[4,1,8192]{2,0,1:T(4,128)(2,1)S(1)} %get-tuple-element.93), channel_id=1, source_target_pairs={{0,1},{1,2},{2,3},{3,4},{4,5},{5,6},{6,7},{8,9},{9,10},{10,11},{11... | collective-permute-start | bytes 196616 | tf_op jit(solution)/shard_map/ppermute | solution.py:16
  166.9 13.4 %collective-permute-start.11 = (bf16[4,8,8192]{2,1,0:T(8,128)(2,1)S(1)}, bf16[4,8,8192]{2,1,0:T(8,128)(2,1)S(1)}, u32[]{:S(2)}, u32[]{:S(2)}) collective-permute-start(bf16[4,8,8192]{2,1,0:T(8,128)(2,1)S(1)} %convert_element_type.223), channel_id=1, source_target_pairs={{0,8},{8,16},{16,24},{24,0},{1,9},{9,17},{17,25},{25,1},{2,10},{10... | collective-permute-start | bytes 1572872 | tf_op jit(solution)/shard_map/ppermute | solution.py:156
  166.9 13.4 %collective-permute-start.12 = (bf16[4,8,8192]{2,1,0:T(8,128)(2,1)S(1)}, bf16[4,8,8192]{2,1,0:T(8,128)(2,1)S(1)}, u32[]{:S(2)}, u32[]{:S(2)}) collective-permute-start(bf16[4,8,8192]{2,1,0:T(8,128)(2,1)S(1)} %convert_element_type.223), channel_id=1, source_target_pairs={{0,24},{8,0},{16,8},{24,16},{1,25},{9,1},{17,9},{25,17},{2,26},{10... | collective-permute-start | bytes 1572872 | tf_op jit(solution)/shard_map/ppermute | solution.py:161
  168.9 20.0 %copy-start.13 = (f32[4,8,8192]{2,0,1:T(4,128)S(1)}, f32[4,8,8192]{2,0,1:T(4,128)}, u32[]{:S(2)}) copy-start(f32[4,8,8192]{2,0,1:T(4,128)} %get-tuple-element.150) | copy-start | bytes 3145732
  168.9 20.0 %copy-start.41 = (s32[16]{0:T(128)S(1)}, s32[16]{0:T(128)}, u32[]{:S(2)}) copy-start(s32[16]{0:T(128)} %get-tuple-element.26) | copy-start | bytes 196
  168.9 20.0 %copy-start.42 = (s32[16]{0:T(128)S(1)}, s32[16]{0:T(128)}, u32[]{:S(2)}) copy-start(s32[16]{0:T(128)} %get-tuple-element.29) | copy-start | bytes 196
  169.0 20.0 %copy-start.48 = (f32[16]{0:T(128)S(1)}, f32[16]{0:T(128)}, u32[]{:S(2)}) copy-start(f32[16]{0:T(128)} %convert_multiply_fusion.4) | copy-start | bytes 196
  180.3 8.6 %collective-permute-start.13 = (bf16[4,8,8192]{2,1,0:T(8,128)(2,1)S(1)}, bf16[4,8,8192]{2,1,0:T(8,128)(2,1)S(1)}, u32[]{:S(2)}, u32[]{:S(2)}) collective-permute-start(bf16[4,8,8192]{2,1,0:T(8,128)(2,1)S(1)} %collective-permute-done.11), channel_id=1, source_target_pairs={{0,8},{8,16},{16,24},{24,0},{1,9},{9,17},{17,25},{25,1},{2,10},{10... | collective-permute-start | bytes 1572872 | tf_op jit(solution)/shard_map/ppermute | solution.py:156
  189.0 2.6 copy-start.49
  192.0 8.6 %collective-permute-start.15 = (bf16[2,1,8192]{2,0,1:T(2,128)(2,1)S(1)}, bf16[2,1,8192]{2,0,1:T(2,128)(2,1)S(1)}, u32[]{:S(2)}, u32[]{:S(2)}) collective-permute-start(bf16[2,1,8192]{2,0,1:T(2,128)(2,1)S(1)} %get-tuple-element.108), channel_id=1, source_target_pairs={{1,0},{2,1},{3,2},{4,3},{5,4},{6,5},{7,6},{9,8},{10,9},{11,10},{12... | collective-permute-start | bytes 98312 | tf_op jit(solution)/shard_map/ppermute | solution.py:18
  193.3 7.4 %collective-permute-start.14 = (bf16[2,1,8192]{2,0,1:T(2,128)(2,1)S(1)}, bf16[2,1,8192]{2,0,1:T(2,128)(2,1)S(1)}, u32[]{:S(2)}, u32[]{:S(2)}) collective-permute-start(bf16[2,1,8192]{2,0,1:T(2,128)(2,1)S(1)} %get-tuple-element.107), channel_id=1, source_target_pairs={{0,1},{1,2},{2,3},{3,4},{4,5},{5,6},{6,7},{8,9},{9,10},{10,11},{11... | collective-permute-start | bytes 98312 | tf_op jit(solution)/shard_map/ppermute | solution.py:16
  204.6 10.7 %copy-start.1 = (bf16[4,8,8192]{2,0,1:T(4,128)(2,1)S(1)}, bf16[4,8,8192]{2,0,1:T(4,128)(2,1)}, u32[]{:S(2)}) copy-start(bf16[4,8,8192]{2,0,1:T(4,128)(2,1)} %copy-done) | copy-start | bytes 1572868
  208.5 8.0 %collective-permute-start.17 = (bf16[2,1,8192]{2,0,1:T(2,128)(2,1)S(1)}, bf16[2,1,8192]{2,0,1:T(2,128)(2,1)S(1)}, u32[]{:S(2)}, u32[]{:S(2)}) collective-permute-start(bf16[2,1,8192]{2,0,1:T(2,128)(2,1)S(1)} %get-tuple-element.106), channel_id=1, source_target_pairs={{1,0},{2,1},{3,2},{4,3},{5,4},{6,5},{7,6},{9,8},{10,9},{11,10},{12... | collective-permute-start | bytes 98312 | tf_op jit(solution)/shard_map/ppermute | solution.py:18
  209.8 7.0 %collective-permute-start.16 = (bf16[2,1,8192]{2,0,1:T(2,128)(2,1)S(1)}, bf16[2,1,8192]{2,0,1:T(2,128)(2,1)S(1)}, u32[]{:S(2)}, u32[]{:S(2)}) collective-permute-start(bf16[2,1,8192]{2,0,1:T(2,128)(2,1)S(1)} %get-tuple-element.105), channel_id=1, source_target_pairs={{0,1},{1,2},{2,3},{3,4},{4,5},{5,6},{6,7},{8,9},{9,10},{10,11},{11... | collective-permute-start | bytes 98312 | tf_op jit(solution)/shard_map/ppermute | solution.py:16
  220.0 14.5 %copy-start.38 = (s32[8]{0:T(128)S(1)}, s32[8]{0:T(128)}, u32[]{:S(2)}) copy-start(s32[8]{0:T(128)} %get-tuple-element.20) | copy-start | bytes 100
  220.0 14.5 %copy-start.39 = (s32[8]{0:T(128)S(1)}, s32[8]{0:T(128)}, u32[]{:S(2)}) copy-start(s32[8]{0:T(128)} %get-tuple-element.21) | copy-start | bytes 100
  220.0 14.5 %copy-start.47 = (f32[8]{0:T(128)S(1)}, f32[8]{0:T(128)}, u32[]{:S(2)}) copy-start(f32[8]{0:T(128)} %convert_multiply_fusion.3) | copy-start | bytes 100
  220.0 8.6 %collective-permute-start.18 = (bf16[2,8,8192]{2,1,0:T(8,128)(2,1)S(1)}, bf16[2,8,8192]{2,1,0:T(8,128)(2,1)S(1)}, u32[]{:S(2)}, u32[]{:S(2)}) collective-permute-start(bf16[2,8,8192]{2,1,0:T(8,128)(2,1)S(1)} %convert_element_type.233), channel_id=1, source_target_pairs={{0,8},{8,16},{16,24},{24,0},{1,9},{9,17},{17,25},{25,1},{2,10},{10... | collective-permute-start | bytes 786440 | tf_op jit(solution)/shard_map/ppermute | solution.py:156
  220.1 8.6 %collective-permute-start.19 = (bf16[2,8,8192]{2,1,0:T(8,128)(2,1)S(1)}, bf16[2,8,8192]{2,1,0:T(8,128)(2,1)S(1)}, u32[]{:S(2)}, u32[]{:S(2)}) collective-permute-start(bf16[2,8,8192]{2,1,0:T(8,128)(2,1)S(1)} %convert_element_type.233), channel_id=1, source_target_pairs={{0,24},{8,0},{16,8},{24,16},{1,25},{9,1},{17,9},{25,17},{2,26},{10... | collective-permute-start | bytes 786440 | tf_op jit(solution)/shard_map/ppermute | solution.py:161
  228.6 5.8 %collective-permute-start.20 = (bf16[2,8,8192]{2,1,0:T(8,128)(2,1)S(1)}, bf16[2,8,8192]{2,1,0:T(8,128)(2,1)S(1)}, u32[]{:S(2)}, u32[]{:S(2)}) collective-permute-start(bf16[2,8,8192]{2,1,0:T(8,128)(2,1)S(1)} %collective-permute-done.18), channel_id=1, source_target_pairs={{0,8},{8,16},{16,24},{24,0},{1,9},{9,17},{17,25},{25,1},{2,10},{10... | collective-permute-start | bytes 786440 | tf_op jit(solution)/shard_map/ppermute | solution.py:156
  236.5 7.7 %collective-permute-start.22 = (bf16[1,1,8192]{2,1,0:T(2,128)(2,1)S(1)}, bf16[1,1,8192]{2,1,0:T(2,128)(2,1)S(1)}, u32[]{:S(2)}, u32[]{:S(2)}) collective-permute-start(bf16[1,1,8192]{2,1,0:T(2,128)(2,1)S(1)} %get-tuple-element.140), channel_id=1, source_target_pairs={{1,0},{2,1},{3,2},{4,3},{5,4},{6,5},{7,6},{9,8},{10,9},{11,10},{12... | collective-permute-start | bytes 49160 | tf_op jit(solution)/shard_map/ppermute | solution.py:18
  237.8 7.0 %collective-permute-start.21 = (bf16[1,1,8192]{2,1,0:T(2,128)(2,1)S(1)}, bf16[1,1,8192]{2,1,0:T(2,128)(2,1)S(1)}, u32[]{:S(2)}, u32[]{:S(2)}) collective-permute-start(bf16[1,1,8192]{2,1,0:T(2,128)(2,1)S(1)} %get-tuple-element.139), channel_id=1, source_target_pairs={{0,1},{1,2},{2,3},{3,4},{4,5},{5,6},{6,7},{8,9},{9,10},{10,11},{11... | collective-permute-start | bytes 49160 | tf_op jit(solution)/shard_map/ppermute | solution.py:16
  250.8 9.3 %collective-permute-start.24 = (bf16[1,1,8192]{2,1,0:T(2,128)(2,1)}, bf16[1,1,8192]{2,1,0:T(2,128)(2,1)}, u32[]{:S(2)}, u32[]{:S(2)}) collective-permute-start(bf16[1,1,8192]{2,1,0:T(2,128)(2,1)} %get-tuple-element.138), channel_id=1, source_target_pairs={{1,0},{2,1},{3,2},{4,3},{5,4},{6,5},{7,6},{9,8},{10,9},{11,10},{12... | collective-permute-start | bytes 49160 | tf_op jit(solution)/shard_map/ppermute | solution.py:18
  252.1 8.9 %collective-permute-start.23 = (bf16[1,1,8192]{2,1,0:T(2,128)(2,1)}, bf16[1,1,8192]{2,1,0:T(2,128)(2,1)}, u32[]{:S(2)}, u32[]{:S(2)}) collective-permute-start(bf16[1,1,8192]{2,1,0:T(2,128)(2,1)} %get-tuple-element.137), channel_id=1, source_target_pairs={{0,1},{1,2},{2,3},{3,4},{4,5},{5,6},{6,7},{8,9},{9,10},{10,11},{11... | collective-permute-start | bytes 49160 | tf_op jit(solution)/shard_map/ppermute | solution.py:16
  259.8 2.6 copy-start.23
  262.9 9.2 %copy-start.44 = (s32[4]{0:T(128)S(1)}, s32[4]{0:T(128)}, u32[]{:S(2)}) copy-start(s32[4]{0:T(128)} %get-tuple-element.16) | copy-start | bytes 52
  262.9 9.2 %copy-start.45 = (s32[4]{0:T(128)S(1)}, s32[4]{0:T(128)}, u32[]{:S(2)}) copy-start(s32[4]{0:T(128)} %get-tuple-element.17) | copy-start | bytes 52
  262.9 9.2 %copy-start.52 = (f32[4]{0:T(128)S(1)}, f32[4]{0:T(128)}, u32[]{:S(2)}) copy-start(f32[4]{0:T(128)} %convert_multiply_fusion.2) | copy-start | bytes 52
  263.2 4.4 %collective-permute-start.25 = (bf16[1,8,8192]{2,1,0:T(8,128)(2,1)S(1)}, bf16[1,8,8192]{2,1,0:T(8,128)(2,1)S(1)}, u32[]{:S(2)}, u32[]{:S(2)}) collective-permute-start(bf16[1,8,8192]{2,1,0:T(8,128)(2,1)S(1)} %convert_element_type.244), channel_id=1, source_target_pairs={{0,8},{8,16},{16,24},{24,0},{1,9},{9,17},{17,25},{25,1},{2,10},{10... | collective-permute-start | bytes 393224 | tf_op jit(solution)/shard_map/ppermute | solution.py:156
  263.3 4.8 %collective-permute-start.26 = (bf16[1,8,8192]{2,1,0:T(8,128)(2,1)S(1)}, bf16[1,8,8192]{2,1,0:T(8,128)(2,1)S(1)}, u32[]{:S(2)}, u32[]{:S(2)}) collective-permute-start(bf16[1,8,8192]{2,1,0:T(8,128)(2,1)S(1)} %convert_element_type.244), channel_id=1, source_target_pairs={{0,24},{8,0},{16,8},{24,16},{1,25},{9,1},{17,9},{25,17},{2,26},{10... | collective-permute-start | bytes 393224 | tf_op jit(solution)/shard_map/ppermute | solution.py:161
  267.7 4.4 %collective-permute-start.27 = (bf16[1,8,8192]{2,1,0:T(8,128)(2,1)S(1)}, bf16[1,8,8192]{2,1,0:T(8,128)(2,1)S(1)}, u32[]{:S(2)}, u32[]{:S(2)}) collective-permute-start(bf16[1,8,8192]{2,1,0:T(8,128)(2,1)S(1)} %collective-permute-done.25), channel_id=1, source_target_pairs={{0,8},{8,16},{16,24},{24,0},{1,9},{9,17},{17,25},{25,1},{2,10},{10... | collective-permute-start | bytes 393224 | tf_op jit(solution)/shard_map/ppermute | solution.py:156
  273.6 1.8 copy-start.17
  273.7 1.8 copy-start.18
  421.1 2.5 copy-start.11
  (22 other events, 24.4 us)
Sparse Core Ops, SparseCore 0:
  281.7 139.2 all-reduce.37
